TPU v7x, 256 devices: a whole 4x4x8 slice. The times are simulated.
256 devices in a mesh: grp: 8 (over x, core), seq: 32 (over z, y).
Axes of the slice: x: 4, y: 4, z: 8, core: 2. Of those that a mesh axis runs over, the one named last changes fastest.
Arguments:
- queries: bfloat16 [8, 3, 32, 128, 512], P('grp', None, 'seq'), may hold values from -120 to 120
- key_input: bfloat16 [8, 3, 32, 128, 512], P('grp', None, 'seq'), may hold values from -8 to 8
- value_input: bfloat16 [8, 3, 32, 128, 512], P('grp', None, 'seq'), may hold values from -6 to 6
- grad_output: bfloat16 [8, 3, 32, 128, 512], P('grp', None, 'seq'), may hold values from -6 to 6
- block_lists: int32 [768, 16], replicated, may hold values from -1 to 767, as said below
- block_flags: int32 [768, 16], replicated, may hold values from 0 to 1, as said below
Outputs:
- attended: bfloat16 [8, 3, 32, 128, 512], P('grp', None, 'seq')
- grad_queries: bfloat16 [8, 3, 32, 128, 512], P('grp', None, 'seq')
- grad_keys: bfloat16 [8, 3, 32, 128, 512], P('grp', None, 'seq')
- grad_values: bfloat16 [8, 3, 32, 128, 512], P('grp', None, 'seq')
Inputs may be any that keep to these rules, and one draw needn't show every extreme that they name: `block_lists`: entry 0 of row t is t itself; the other used entries of a row are distinct tiles u < t, each either in the same block of 96 tiles as t, or in an earlier block with u % 32 == t % 32; used entries come first and -1 fills the rest. The 3 rows t = (a * 3 + b) * 32 + c that share a and c name together at most one tile of the form (a2 * 3 + b2) * 32 + c2 for each pair (a2, c2) other than (a, c). block_flags[t, 0] is 1 for every t; a flag whose list entry is -1 has no effect.
All inputs are finite; a program needn't handle non-finite values.
Results may differ from a plain program's by a relative error of at most 0.029.
Values may be sent and summed in bfloat16 or wider, within the bound.
No kernel may reach another device: no remote copies, remote signals or barrier semaphores. Data moves between devices by JAX's collectives and lax.ppermute only.
A program may use at most 256 MiB of HBM per device.

v0:
```python
import jax
import jax.numpy as jnp
from jax import lax
from jax.sharding import PartitionSpec as P

HEADS = 8
HEAD_DIM = 64
floor_score = -1e30


def locate(entry_ids, group_tiles, columns):
    safe_ids = jnp.maximum(entry_ids, 0)
    within = safe_ids % group_tiles
    return (safe_ids // group_tiles, within // columns, within % columns)


def per_device(queries, key_input, value_input, grad_output, block_lists, block_flags):
    tile_dev = queries.shape[1]
    tile_rows = queries.shape[3]
    width = queries.shape[4]
    entries = block_lists.shape[1]
    columns = lax.axis_size("seq")
    groups = lax.axis_size("grp")
    group_at = lax.axis_index("grp")
    column_at = lax.axis_index("seq")
    group_tiles = tile_dev * columns
    query_tiles = queries.reshape(tile_dev, tile_rows, width)
    key_tiles = key_input.reshape(tile_dev, tile_rows, width)
    value_tiles = value_input.reshape(tile_dev, tile_rows, width)
    grad_tiles = grad_output.reshape(tile_dev, tile_rows, width)
    ranks = jnp.arange(tile_dev, dtype=jnp.int32)
    column_ids = jnp.arange(columns, dtype=jnp.int32)
    group_ids = jnp.arange(groups, dtype=jnp.int32)
    my_tiles = (group_at * tile_dev + ranks) * columns + column_at
    my_lists = jnp.take(block_lists, my_tiles, axis=0)
    my_flags = jnp.take(block_flags, my_tiles, axis=0)
    present = my_lists >= 0
    owner_group, owner_rank, owner_column = locate(my_lists, group_tiles, columns)
    same_group = owner_group == group_at
    is_own = present & same_group & (owner_column == column_at)
    is_near = present & same_group & (owner_column != column_at)
    is_far = present & jnp.logical_not(same_group)
    group_rows = lax.dynamic_slice_in_dim(block_lists, group_at * group_tiles, group_tiles, 0)
    group_rows = group_rows.reshape(tile_dev, columns, entries)
    row_group, row_rank, row_column = locate(group_rows, group_tiles, columns)
    named_here = (group_rows >= 0) & (row_group == group_at) & (row_column == column_at)
    near_rank = jnp.max(jnp.where(named_here, row_rank, -1), axis=(0, 2))
    near_rank = jnp.where(column_ids == column_at, -1, near_rank)
    column_rows = jnp.take(
        block_lists.reshape(groups, tile_dev, columns, entries), column_at, axis=2
    )
    far_group, far_rank_all, far_column = locate(column_rows, group_tiles, columns)
    named_far = (column_rows >= 0) & (far_group == group_at) & (far_column == column_at)
    far_rank = jnp.max(jnp.where(named_far, far_rank_all, -1), axis=(1, 2))
    far_rank = jnp.where(group_ids == group_at, -1, far_rank)
    wanted = jnp.max(
        jnp.where(
            is_near[:, :, None] & (owner_column[:, :, None] == column_ids),
            owner_rank[:, :, None],
            -1,
        ),
        axis=(0, 1),
    )
    pieces = (
        lax.all_gather(key_tiles, "seq", axis=0, tiled=True),
        lax.all_gather(value_tiles, "seq", axis=0, tiled=True),
    )
    span_rows = pieces[0].shape[0]
    row_at = jnp.arange(span_rows, dtype=jnp.int32)
    select = (
        (row_at[None, :] // tile_dev == column_ids[:, None])
        & (row_at[None, :] % tile_dev == wanted[:, None])
    ).astype(jnp.bfloat16)
    new_keys = jnp.einsum("pn,ntw->ptw", select, pieces[0], preferred_element_type=jnp.float32)
    new_values = jnp.einsum("pn,ntw->ptw", select, pieces[1], preferred_element_type=jnp.float32)
    near_keys = new_keys.astype(jnp.bfloat16)
    near_values = new_values.astype(jnp.bfloat16)
    far_out = jnp.maximum(far_rank, 0)
    far_keys, far_values = (
        lax.all_to_all(
            jnp.take(key_tiles, far_out, axis=0), "grp", split_axis=0, concat_axis=0, tiled=True
        ),
        lax.all_to_all(
            jnp.take(value_tiles, far_out, axis=0), "grp", split_axis=0, concat_axis=0, tiled=True
        ),
    )
    own_slot = jnp.where(is_own, owner_rank, 0)
    near_slot = jnp.where(is_near, owner_column, 0)
    far_slot = jnp.where(is_far, owner_group, 0)
    own_pick = is_own[:, :, None, None]
    near_pick = is_near[:, :, None, None]
    far_pick = is_far[:, :, None, None]
    pair_width = 2 * HEAD_DIM
    score_scale = HEAD_DIM ** (-0.5)
    positions = jnp.arange(tile_rows)
    lower_mask = positions[None, :] <= positions[:, None]
    allowed = present[:, None, :, None] & (
        (my_flags == 0)[:, None, :, None] | lower_mask[None, :, None, :]
    )

    def spread(term, chosen_pick, slot, slots):
        total = jnp.zeros((slots, tile_rows, pair_width), jnp.float32)
        return total.at[slot].add(jnp.where(chosen_pick, term, 0.0)).astype(jnp.bfloat16)

    attended_parts = []
    query_parts = []
    own_key_parts = []
    near_key_parts = []
    far_key_parts = []
    own_value_parts = []
    near_value_parts = []
    far_value_parts = []
    for head_pair in range(HEADS // 2):
        start_col = head_pair * pair_width

        def columns_of(source):
            return source[..., start_col : start_col + pair_width]

        def fetch(own_source, near_source, far_source):
            from_own = jnp.take(columns_of(own_source), own_slot, axis=0)
            from_near = jnp.take(columns_of(near_source), near_slot, axis=0)
            from_far = jnp.take(columns_of(far_source), far_slot, axis=0)
            return jnp.where(own_pick, from_own, jnp.where(near_pick, from_near, from_far))

        key_block = fetch(key_tiles, near_keys, far_keys).reshape(
            tile_dev, entries, tile_rows, 2, HEAD_DIM
        )
        value_block = fetch(value_tiles, near_values, far_values).reshape(
            tile_dev, entries, tile_rows, 2, HEAD_DIM
        )
        query_block = columns_of(query_tiles).reshape(tile_dev, tile_rows, 2, HEAD_DIM)
        grad_block = columns_of(grad_tiles).reshape(tile_dev, tile_rows, 2, HEAD_DIM)
        scores = (
            jnp.einsum(
                "tihd,techd->thiec", query_block, key_block, preferred_element_type=jnp.float32
            )
            * score_scale
        )
        masked = jnp.where(allowed[:, None], scores, floor_score)
        row_top = jnp.max(masked, axis=(3, 4), keepdims=True)
        exponent = jnp.exp(masked - row_top)
        probs_exact = exponent / jnp.sum(exponent, axis=(3, 4), keepdims=True)
        probs = probs_exact.astype(jnp.bfloat16)
        attended_block = jnp.einsum(
            "thiec,techd->tihd", probs, value_block, preferred_element_type=jnp.float32
        ).astype(jnp.bfloat16)
        row_delta = jnp.sum(
            grad_block.astype(jnp.float32) * attended_block.astype(jnp.float32), axis=3
        )
        dprobs = jnp.einsum(
            "tihd,techd->thiec", grad_block, value_block, preferred_element_type=jnp.float32
        )
        dscores = (
            probs_exact * (dprobs - jnp.transpose(row_delta, (0, 2, 1))[..., None, None])
        ).astype(jnp.bfloat16)
        grad_query = (
            jnp.einsum("thiec,techd->tihd", dscores, key_block, preferred_element_type=jnp.float32)
            * score_scale
        )
        grad_key = (
            jnp.einsum(
                "thiec,tihd->techd", dscores, query_block, preferred_element_type=jnp.float32
            )
            * score_scale
        )
        grad_value = jnp.einsum(
            "thiec,tihd->techd", probs, grad_block, preferred_element_type=jnp.float32
        )
        grad_key = grad_key.reshape(tile_dev, entries, tile_rows, pair_width)
        grad_value = grad_value.reshape(tile_dev, entries, tile_rows, pair_width)
        attended_parts.append(attended_block.reshape(tile_dev, tile_rows, pair_width))
        query_parts.append(grad_query.astype(jnp.bfloat16).reshape(tile_dev, tile_rows, pair_width))
        own_key_parts.append(spread(grad_key, own_pick, own_slot, tile_dev))
        near_key_parts.append(spread(grad_key, near_pick, near_slot, columns))
        far_key_parts.append(spread(grad_key, far_pick, far_slot, groups))
        own_value_parts.append(spread(grad_value, own_pick, own_slot, tile_dev))
        near_value_parts.append(spread(grad_value, near_pick, near_slot, columns))
        far_value_parts.append(spread(grad_value, far_pick, far_slot, groups))

    def joined(parts):
        return jnp.concatenate(parts, axis=-1)

    near_back_keys, near_back_values = (
        lax.all_to_all(joined(near_key_parts), "seq", split_axis=0, concat_axis=0, tiled=True),
        lax.all_to_all(joined(near_value_parts), "seq", split_axis=0, concat_axis=0, tiled=True),
    )
    far_back_keys, far_back_values = (
        lax.all_to_all(joined(far_key_parts), "grp", split_axis=0, concat_axis=0, tiled=True),
        lax.all_to_all(joined(far_value_parts), "grp", split_axis=0, concat_axis=0, tiled=True),
    )
    near_onehot = (near_rank[None, :] == ranks[:, None]).astype(jnp.bfloat16)
    far_onehot = (far_rank[None, :] == ranks[:, None]).astype(jnp.bfloat16)

    def collect(own_part, near_back, far_back):
        total = own_part.astype(jnp.float32)
        total = total + jnp.einsum(
            "rp,ptw->rtw", near_onehot, near_back, preferred_element_type=jnp.float32
        )
        total = total + jnp.einsum(
            "rg,gtw->rtw", far_onehot, far_back, preferred_element_type=jnp.float32
        )
        return total.astype(jnp.bfloat16).reshape(1, tile_dev, 1, tile_rows, width)

    attended = joined(attended_parts).reshape(1, tile_dev, 1, tile_rows, width)
    grad_queries = joined(query_parts).reshape(1, tile_dev, 1, tile_rows, width)
    grad_keys = collect(joined(own_key_parts), near_back_keys, far_back_keys)
    grad_values = collect(joined(own_value_parts), near_back_values, far_back_values)
    return (attended, grad_queries, grad_keys, grad_values)


def solution(mesh):
    return jax.shard_map(
        per_device,
        mesh=mesh,
        in_specs=(
            P("grp", None, "seq", None, None),
            P("grp", None, "seq", None, None),
            P("grp", None, "seq", None, None),
            P("grp", None, "seq", None, None),
            P(),
            P(),
        ),
        out_specs=(
            P("grp", None, "seq", None, None),
            P("grp", None, "seq", None, None),
            P("grp", None, "seq", None, None),
            P("grp", None, "seq", None, None),
        ),
        check_vma=False,
    )
```

profile of v0, /device:TPU:1, one launch (start us, length us, event | category | flops | bytes accessed | tf_op | source)
XLA Modules:
  0.0 858.7 jit_solution(12798939972070502319)
XLA Ops:
  17.0 6.8 all-to-all-start
  29.0 10.0 %all-to-all-done = bf16[8,128,512]{2,1,0:T(8,128)(2,1)S(1)} async-done(((bf16[8,128,512]{2,1,0:T(8,128)(2,1)}), bf16[8,128,512]{2,1,0:T(8,128)(2,1)S(1)}, u32[]{:S(2)}, u32[]{:S(2)}) %all-to-all-start) | async-done | bytes 1048608 | tf_op jit(solution)/shard_map/all_to_all | solution.py:83
  39.0 5.0 all-to-all-start.1
  126.1 7.6 all-gather.5.cloned.1.call-done
  133.7 19.3 %fusion.26 = bf16[32,128,512]{2,0,1:T(8,128)(2,1)S(1)} fusion(bf16[1,96,1,128,512]{4,3,2,0,1:T(8,128)(2,1)} %all-gather.5.cloned.1.call-done, s32[96]{0:T(128)S(1)} %get-tuple-element.179, s32[96]{0:T(128)S(1)} %copy-done.72, s32[32]{0:T(128)S(1)} %select_reduce_fusion), kind=kOutput, calls=%fused_computation.121 | convolution fusion | flops 404759552 | bytes 16778112 | tf_op jit(solution)/shard_map/pn,ntw->ptw/dot_general | solution.py:75
  160.2 92.9 %all-gather.7.cloned.1.call-done = bf16[1,96,1,128,512]{4,3,2,0,1:T(8,128)(2,1)} async-done(((bf16[1,3,1,128,512]{4,3,2,0,1:T(8,128)(2,1)}), bf16[1,96,1,128,512]{4,3,2,0,1:T(8,128)(2,1)}) %all-gather.7.cloned.1.call-update) | async-done | bytes 12582928 | tf_op jit(solution)/shard_map/all_gather | solution.py:65
  253.1 19.1 %fusion.29 = bf16[32,128,512]{2,0,1:T(8,128)(2,1)S(1)} fusion(bf16[1,96,1,128,512]{4,3,2,0,1:T(8,128)(2,1)} %all-gather.7.cloned.1.call-done, s32[96]{0:T(128)S(1)} %get-tuple-element.179, s32[96]{0:T(128)S(1)} %copy-done.72, s32[32]{0:T(128)S(1)} %select_reduce_fusion), kind=kOutput, calls=%fused_computation.122 | convolution fusion | flops 404759552 | bytes 16778112 | tf_op jit(solution)/shard_map/pn,ntw->ptw/dot_general | solution.py:74
  316.8 8.7 %fusion.35 = (bf16[3,16,128,128]{2,3,1,0:T(8,128)(2,1)}, bf16[3,16,128,128]{2,3,1,0:T(8,128)(2,1)S(1)}, bf16[3,16,128,128]{2,3,1,0:T(8,128)(2,1)}, bf16[3,16,128,128]{2,3,1,0:T(8,128)(2,1)S(1)}) fusion(bf16[3,16,128,128]{2,3,1,0:T(8,128)(2,1)} %bitcast.460, bf16[3,16,128,128]{2,3,1,0:T(8,128)(2,1)} %copy.966, bf16[3,16,128,128]{2,3,1,0:T(8,128)(2,1)S(1)} %bitcast.452, ...), kind=kLoop, calls=%fused_computation.134 | loop fusion | flops 15728640 | bytes 25166064 | tf_op jit(solution)/shard_map/jit(_where)/select_n | solution.py:123
  331.0 4.9 fusion.39
  335.9 6.2 fusion.18
  342.2 6.1 fusion.11
  348.3 4.0 fusion.13
  385.5 4.8 fusion.9
  409.9 32.1 %bitcast_select_fusion.18 = (f32[3,16,128,128]{2,3,1,0:T(8,128)}, f32[3,16,128,128]{2,3,1,0:T(8,128)}, f32[3,16,128,128]{2,3,1,0:T(8,128)}, f32[3,16,128,128]{2,...) fusion(f32[3,16,128,2,64]{2,4,3,1,0:T(8,128)S(1)} %copy.1022, ...), kind=kLoop, calls=%fused_computation.106 | loop fusion | flops 18874368 | bytes 100663440 | tf_op jit(solution)/shard_map/jit(_where)/select_n | solution.py:103
  445.7 7.1 scatter_fusion.11
  452.8 3.6 copy.1032
  456.5 6.7 scatter_fusion.10
  463.9 3.6 copy.1031
  467.6 6.7 scatter_fusion.9
  478.7 6.7 scatter_fusion.8
  487.7 5.3 all-to-all-start.3
  495.4 6.7 scatter_fusion.23
  505.7 6.7 scatter_fusion.22
  513.2 3.7 copy.1055
  517.0 6.7 scatter_fusion.21
  528.0 6.7 scatter_fusion.20
  537.1 5.0 all-to-all-start.5
  544.8 6.7 scatter_fusion.7
  555.5 6.7 scatter_fusion.6
  567.2 6.7 scatter_fusion.5
  578.8 6.7 scatter_fusion.4
  589.3 5.8 all-to-all-start.2
  597.8 6.7 scatter_fusion.19
  608.5 6.7 scatter_fusion.18
  620.1 6.7 scatter_fusion.17
  631.8 6.7 scatter_fusion.16
  642.3 45.9 %all-to-all-done.2 = bf16[32,128,512]{2,1,0:T(8,128)(2,1)} async-done(((bf16[32,128,512]{2,1,0:T(8,128)(2,1)}), bf16[32,128,512]{2,1,0:T(8,128)(2,1)}, u32[]{:S(2)}, u32[]{:S(2)}) %all-to-all-start.2) | async-done | bytes 4194336 | tf_op jit(solution)/shard_map/all_to_all | solution.py:184
  688.3 9.9 %all-to-all-start.4 = ((bf16[32,128,512]{2,1,0:T(8,128)(2,1)}), bf16[32,128,512]{2,1,0:T(8,128)(2,1)}, u32[]{:S(2)}, u32[]{:S(2)}) async-start(bf16[32,128,512]{2,1,0:T(8,128)(2,1)} %pad_maximum_fusion.1), calls=%async_computation.4 | async-start | bytes 8388608 | tf_op jit(solution)/shard_map/all_to_all | solution.py:185
  719.1 10.2 %scatter_fusion.3 = f32[3,128,128]{2,1,0:T(8,128)} fusion(f32[3,128,128]{2,1,0:T(8,128)} %broadcast.258.clone, s32[48]{0:T(128)S(1)} %copy-done.41, f32[48,128,128]{2,1,0:T(8,128)S(1)} %copy.1023), kind=kCustom, calls=%fused_computation.31 | custom fusion | flops 786432 | bytes 9437376 | tf_op jit(solution)/shard_map/scatter-add | solution.py:103
  733.4 10.2 %scatter_fusion.2 = f32[3,128,128]{2,1,0:T(8,128)} fusion(f32[3,128,128]{2,1,0:T(8,128)} %broadcast.258.clone.1, s32[48]{0:T(128)S(1)} %copy-done.41, f32[48,128,128]{2,1,0:T(8,128)S(1)} %copy.1020), kind=kCustom, calls=%fused_computation.30 | custom fusion | flops 786432 | bytes 9437376 | tf_op jit(solution)/shard_map/scatter-add | solution.py:103
  747.6 10.2 %scatter_fusion.1 = f32[3,128,128]{2,1,0:T(8,128)} fusion(f32[3,128,128]{2,1,0:T(8,128)} %broadcast.258.clone.2, s32[48]{0:T(128)S(1)} %copy-done.41, f32[48,128,128]{2,1,0:T(8,128)S(1)} %copy.1017), kind=kCustom, calls=%fused_computation.29 | custom fusion | flops 786432 | bytes 9437376 | tf_op jit(solution)/shard_map/scatter-add | solution.py:103
  761.8 10.2 %scatter_fusion = f32[3,128,128]{2,1,0:T(8,128)} fusion(f32[3,128,128]{2,1,0:T(8,128)} %broadcast.258.clone.3, s32[48]{0:T(128)S(1)} %copy-done.41, f32[48,128,128]{2,1,0:T(8,128)S(1)} %copy.1014), kind=kCustom, calls=%fused_computation.28 | custom fusion | flops 786432 | bytes 9437376 | tf_op jit(solution)/shard_map/scatter-add | solution.py:103
  776.7 10.2 %scatter_fusion.15 = f32[3,128,128]{2,1,0:T(8,128)} fusion(f32[3,128,128]{2,1,0:T(8,128)} %broadcast.258.clone.4, s32[48]{0:T(128)S(1)} %copy-done.41, f32[48,128,128]{2,1,0:T(8,128)S(1)} %copy.1047), kind=kCustom, calls=%fused_computation.43 | custom fusion | flops 786432 | bytes 9437376 | tf_op jit(solution)/shard_map/scatter-add | solution.py:103
  791.0 10.2 %scatter_fusion.14 = f32[3,128,128]{2,1,0:T(8,128)} fusion(f32[3,128,128]{2,1,0:T(8,128)} %broadcast.258.clone.5, s32[48]{0:T(128)S(1)} %copy-done.41, f32[48,128,128]{2,1,0:T(8,128)S(1)} %copy.1044), kind=kCustom, calls=%fused_computation.42 | custom fusion | flops 786432 | bytes 9437376 | tf_op jit(solution)/shard_map/scatter-add | solution.py:103
  805.8 10.2 %scatter_fusion.13 = f32[3,128,128]{2,1,0:T(8,128)} fusion(f32[3,128,128]{2,1,0:T(8,128)} %broadcast.258.clone.6, s32[48]{0:T(128)S(1)} %copy-done.41, f32[48,128,128]{2,1,0:T(8,128)S(1)} %copy.1041), kind=kCustom, calls=%fused_computation.41 | custom fusion | flops 786432 | bytes 9437376 | tf_op jit(solution)/shard_map/scatter-add | solution.py:103
  820.9 10.2 %scatter_fusion.12 = f32[3,128,128]{2,1,0:T(8,128)} fusion(f32[3,128,128]{2,1,0:T(8,128)} %broadcast.258.clone.7, s32[48]{0:T(128)S(1)} %copy-done.41, f32[48,128,128]{2,1,0:T(8,128)S(1)} %copy.1038), kind=kCustom, calls=%fused_computation.40 | custom fusion | flops 786432 | bytes 9437376 | tf_op jit(solution)/shard_map/scatter-add | solution.py:103
  839.7 4.6 fusion.24
  845.6 4.6 fusion.22
  (383 shorter events, 333.4 us)
Async XLA Ops:
  7.2 5.2 copy-start.12
  7.2 126.5 %all-gather.5.cloned.1.call-start = ((), (), s32[]{:S(2)}) async-start(), calls=%async_computation.6 | async-start | bytes 12976128 | tf_op jit(solution)/shard_map/all_gather | solution.py:66
  7.9 245.2 %all-gather.7.cloned.1.call-start = ((), (), s32[]{:S(2)}) async-start(), calls=%async_computation.7 | async-start | bytes 12976128 | tf_op jit(solution)/shard_map/all_gather | solution.py:65
  14.0 9.8 %copy-start.56 = (s32[768,16]{0,1:T(8,128)S(1)}, s32[768,16]{0,1:T(8,128)}, u32[]{:S(2)}) copy-start(s32[768,16]{0,1:T(8,128)} %param.20) | copy-start | bytes 147460
  14.0 10.0 %copy-start.65 = (s32[768,16]{0,1:T(8,128)S(1)}, s32[768,16]{0,1:T(8,128)}, u32[]{:S(2)}) copy-start(s32[768,16]{0,1:T(8,128)} %param.21) | copy-start | bytes 147460
  14.0 13.3 %copy-start.13 = (bf16[1,3,1,128,512]{4,3,2,1,0:T(8,128)(2,1)S(1)}, bf16[1,3,1,128,512]{4,3,2,1,0:T(8,128)(2,1)}, u32[]{:S(2)}) copy-start(bf16[1,3,1,128,512]{4,3,2,1,0:T(8,128)(2,1)} %param.17) | copy-start | bytes 1179652
  17.0 10.4 %copy-start.51 = (bf16[1,3,1,128,512]{4,3,2,1,0:T(8,128)(2,1)S(1)}, bf16[1,3,1,128,512]{4,3,2,1,0:T(8,128)(2,1)}, u32[]{:S(2)}) copy-start(bf16[1,3,1,128,512]{4,3,2,1,0:T(8,128)(2,1)} %param.19) | copy-start | bytes 1179652
  17.0 11.2 %copy-start.52 = (bf16[1,3,1,128,512]{4,3,2,1,0:T(8,128)(2,1)S(1)}, bf16[1,3,1,128,512]{4,3,2,1,0:T(8,128)(2,1)}, u32[]{:S(2)}) copy-start(bf16[1,3,1,128,512]{4,3,2,1,0:T(8,128)(2,1)} %param.16) | copy-start | bytes 1179652
  17.0 21.9 %all-to-all-start = ((bf16[8,128,512]{2,1,0:T(8,128)(2,1)}), bf16[8,128,512]{2,1,0:T(8,128)(2,1)S(1)}, u32[]{:S(2)}, u32[]{:S(2)}) async-start(bf16[8,128,512]{2,1,0:T(8,128)(2,1)} %get-tuple-element.167), calls=%async_computation | async-start | bytes 2097152 | tf_op jit(solution)/shard_map/all_to_all | solution.py:83
  26.0 302.3 %copy-start.68 = (pred[3,16]{1,0:T(4,128)(4,1)}, pred[3,16]{1,0:T(4,128)(4,1)S(1)}, u32[]{:S(2)}) copy-start(pred[3,16]{1,0:T(4,128)(4,1)S(1)} %get-tuple-element.61) | copy-start | bytes 148
  26.5 301.8 %copy-start.66 = (pred[3,16]{1,0:T(4,128)(4,1)}, pred[3,16]{1,0:T(4,128)(4,1)S(1)}, u32[]{:S(2)}) copy-start(pred[3,16]{1,0:T(4,128)(4,1)S(1)} %get-tuple-element.69) | copy-start | bytes 148
  39.0 11.1 %copy-start.24 = (bf16[8,128,512]{2,1,0:T(8,128)(2,1)}, bf16[8,128,512]{2,1,0:T(8,128)(2,1)S(1)}, u32[]{:S(2)}) copy-start(bf16[8,128,512]{2,1,0:T(8,128)(2,1)S(1)} %all-to-all-done) | copy-start | bytes 3145732
  39.0 53.7 %all-to-all-start.1 = ((bf16[8,128,512]{2,1,0:T(8,128)(2,1)}), bf16[8,128,512]{2,1,0:T(8,128)(2,1)}, u32[]{:S(2)}, u32[]{:S(2)}) async-start(bf16[8,128,512]{2,1,0:T(8,128)(2,1)} %get-tuple-element.166), calls=%async_computation.1 | async-start | bytes 2097152 | tf_op jit(solution)/shard_map/all_to_all | solution.py:80
  46.1 38.6 %copy-start.42 = (s32[48]{0:T(128)}, s32[48]{0:T(128)S(1)}, u32[]{:S(2)}) copy-start(s32[48]{0:T(128)S(1)} %reshape.872) | copy-start | bytes 580
  64.1 261.5 %copy-start.36 = (bf16[3,128,128]{1,2,0:T(8,128)(2,1)}, bf16[3,128,128]{1,2,0:T(8,128)(2,1)S(1)}, u32[]{:S(2)}) copy-start(bf16[3,128,128]{1,2,0:T(8,128)(2,1)S(1)} %copy.972) | copy-start | bytes 294916
  75.9 8.1 copy-start.53
  75.9 9.0 %copy-start.73 = (pred[3,16]{1,0:T(4,128)(4,1)S(1)}, pred[3,16]{1,0:T(4,128)(4,1)}, u32[]{:S(2)}) copy-start(pred[3,16]{1,0:T(4,128)(4,1)} %get-tuple-element.165) | copy-start | bytes 148
  76.7 6.5 copy-start.54
  121.4 12.3 %copy-start.72 = (s32[96]{0:T(128)S(1)}, s32[96]{0:T(128)}, u32[]{:S(2)}) copy-start(s32[96]{0:T(128)} %get-tuple-element.180) | copy-start | bytes 1156
  331.0 4.9 copy-start.46
  335.9 6.3 copy-start.14
  335.9 6.3 copy-start.15
  335.9 6.3 copy-start.29
  335.9 6.3 copy-start.47
  362.0 28.3 %copy-start.4 = (bf16[3,2,128,16,128]{2,4,3,1,0:T(8,128)(2,1)}, bf16[3,2,128,16,128]{2,4,3,1,0:T(8,128)(2,1)S(1)}, u32[]{:S(2)}) copy-start(bf16[3,2,128,16,128]{2,4,3,1,0:T(8,128)(2,1)S(1)} %fusion.6) | copy-start | bytes 9437188
  370.4 36.5 %copy-start.5 = (bf16[3,2,128,16,128]{2,4,3,1,0:T(8,128)(2,1)}, bf16[3,2,128,16,128]{2,4,3,1,0:T(8,128)(2,1)S(1)}, u32[]{:S(2)}) copy-start(bf16[3,2,128,16,128]{2,4,3,1,0:T(8,128)(2,1)S(1)} %fusion.7) | copy-start | bytes 9437188
  373.3 6.5 slice-start
  379.9 23.9 %copy-start.6 = (bf16[3,2,128,16,128]{2,4,3,1,0:T(8,128)(2,1)}, bf16[3,2,128,16,128]{2,4,3,1,0:T(8,128)(2,1)S(1)}, u32[]{:S(2)}) copy-start(bf16[3,2,128,16,128]{2,4,3,1,0:T(8,128)(2,1)S(1)} %fusion.8) | copy-start | bytes 9437188
  385.5 4.8 copy-start.39
  390.3 10.4 %copy-start.7 = (bf16[3,2,128,16,128]{2,4,3,1,0:T(8,128)(2,1)}, bf16[3,2,128,16,128]{2,4,3,1,0:T(8,128)(2,1)S(1)}, u32[]{:S(2)}) copy-start(bf16[3,2,128,16,128]{2,4,3,1,0:T(8,128)(2,1)S(1)} %fusion.9) | copy-start | bytes 9437188
  485.4 7.6 copy-start.11
  487.7 49.4 %all-to-all-start.3 = ((bf16[8,128,512]{2,1,0:T(8,128)(2,1)}), bf16[8,128,512]{2,1,0:T(8,128)(2,1)}, u32[]{:S(2)}, u32[]{:S(2)}) async-start(bf16[8,128,512]{2,1,0:T(8,128)(2,1)} %pad_maximum_fusion.2), calls=%async_computation.3 | async-start | bytes 2097152 | tf_op jit(solution)/shard_map/all_to_all | solution.py:188
  534.8 7.4 copy-start.10
  537.1 52.2 %all-to-all-start.5 = ((bf16[8,128,512]{2,1,0:T(8,128)(2,1)}), bf16[8,128,512]{2,1,0:T(8,128)(2,1)}, u32[]{:S(2)}, u32[]{:S(2)}) async-start(bf16[8,128,512]{2,1,0:T(8,128)(2,1)} %pad_maximum_fusion.3), calls=%async_computation.5 | async-start | bytes 2097152 | tf_op jit(solution)/shard_map/all_to_all | solution.py:189
  589.3 5.8 copy-start.9
  589.3 98.9 %all-to-all-start.2 = ((bf16[32,128,512]{2,1,0:T(8,128)(2,1)}), bf16[32,128,512]{2,1,0:T(8,128)(2,1)}, u32[]{:S(2)}, u32[]{:S(2)}) async-start(bf16[32,128,512]{2,1,0:T(8,128)(2,1)} %pad_maximum_fusion), calls=%async_computation.2 | async-start | bytes 8388608 | tf_op jit(solution)/shard_map/all_to_all | solution.py:184
  642.3 57.0 %copy-start.57 = (bf16[3,2,64,128]{3,2,1,0:T(8,128)(2,1)S(1)}, bf16[3,2,64,128]{3,2,1,0:T(8,128)(2,1)}, u32[]{:S(2)}) copy-start(bf16[3,2,64,128]{3,2,1,0:T(8,128)(2,1)} %get-tuple-element.172) | copy-start | bytes 294916
  642.3 57.7 %copy-start.58 = (bf16[3,2,64,128]{3,2,1,0:T(8,128)(2,1)S(1)}, bf16[3,2,64,128]{3,2,1,0:T(8,128)(2,1)}, u32[]{:S(2)}) copy-start(bf16[3,2,64,128]{3,2,1,0:T(8,128)(2,1)} %get-tuple-element.174) | copy-start | bytes 294916
  642.3 58.5 %copy-start.59 = (bf16[3,2,64,128]{3,2,1,0:T(8,128)(2,1)S(1)}, bf16[3,2,64,128]{3,2,1,0:T(8,128)(2,1)}, u32[]{:S(2)}) copy-start(bf16[3,2,64,128]{3,2,1,0:T(8,128)(2,1)} %get-tuple-element.176) | copy-start | bytes 294916
  642.3 59.3 %copy-start.60 = (bf16[3,2,64,128]{3,2,1,0:T(8,128)(2,1)S(1)}, bf16[3,2,64,128]{3,2,1,0:T(8,128)(2,1)}, u32[]{:S(2)}) copy-start(bf16[3,2,64,128]{3,2,1,0:T(8,128)(2,1)} %get-tuple-element.178) | copy-start | bytes 294916
  642.3 60.0 %copy-start.3 = (bf16[3,16,128,128]{2,3,1,0:T(8,128)(2,1)S(1)}, bf16[3,16,128,128]{2,3,1,0:T(8,128)(2,1)}, u32[]{:S(2)}) copy-start(bf16[3,16,128,128]{2,3,1,0:T(8,128)(2,1)} %copy-done.2) | copy-start | bytes 4718596
  688.3 157.3 %all-to-all-start.4 = ((bf16[32,128,512]{2,1,0:T(8,128)(2,1)}), bf16[32,128,512]{2,1,0:T(8,128)(2,1)}, u32[]{:S(2)}, u32[]{:S(2)}) async-start(bf16[32,128,512]{2,1,0:T(8,128)(2,1)} %pad_maximum_fusion.1), calls=%async_computation.4 | async-start | bytes 8388608 | tf_op jit(solution)/shard_map/all_to_all | solution.py:185
  698.2 7.5 copy-start.1
  708.3 4.8 copy-start.8
  820.9 14.8 %copy-start.71 = (s32[8]{0:T(128)S(1)}, s32[8]{0:T(128)}, u32[]{:S(2)}) copy-start(s32[8]{0:T(128)} %copy-done.70) | copy-start | bytes 100
  839.7 4.6 copy-start.48
  845.6 4.7 copy-start.49
  845.6 4.7 copy-start.50
  (37 other events, 89.2 us)
Sparse Core Ops, SparseCore 0:
  10.6 123.0 all-gather.4
  136.3 116.7 all-gather.6
where the time goes:
time: 874 us; the launch traced here: 859 us
  other arithmetic  280 us (32%)
  local copies, waits for them, and re-layouts  247 us (28%)
  waiting for transfers between devices  158 us (18%)
  matrix products  120 us (14%)
  starting transfers between devices  37.9 us (4%)
  between operations  15.9 us (2%)
    scatter-add x24, other arithmetic, spread(): total.at[slot].add(jnp.where(chosen_pick, term, 0.0)).astype(jnp.bfloat16)  190 us
    all_gather x1, waiting for transfers between devices, per_device(): lax.all_gather(key_tiles, 'seq', axis=0, tiled=True)  92.9 us
    select_n x24, local copies, waits for them, and re-layouts, spread(): jnp.where(chosen_pick, term, 0.0)  72.8 us
    all_to_all x1, waiting for transfers between devices, per_device(): lax.all_to_all(joined(near_key_parts), 'seq', split_axis=0, concat_axis=0...  45.9 us
    gather x16, local copies, waits for them, and re-layouts, fetch(): from_near = jnp.take(columns_of(near_source), near_slot, axis=0)  36.9 us
    gather x16, local copies, waits for them, and re-layouts, fetch(): from_far = jnp.take(columns_of(far_source), far_slot, axis=0)  36.7 us
    select_n x1, other arithmetic, spread(): jnp.where(chosen_pick, term, 0.0)  32.1 us
    gather x16, local copies, waits for them, and re-layouts, fetch(): from_own = jnp.take(columns_of(own_source), own_slot, axis=0)  32 us
  transfers between devices with their start and end apart: 8, of which 4 were waited for; matrix products, arithmetic and copies ran while one was open for 47% of the time, Pallas kernels for 0%

commit v1 on v0

--- a/solution.py
+++ b/solution.py
@@ -62,7 +62,9 @@
         axis=(0, 1),
     )
     pieces = (
-        lax.all_gather(key_tiles, "seq", axis=0, tiled=True),
+        jnp.concatenate(
+            lax.all_to_all(jnp.stack([key_tiles] * lax.axis_size("seq")), "seq", 0, 0), axis=0
+        ),
         lax.all_gather(value_tiles, "seq", axis=0, tiled=True),
     )
     span_rows = pieces[0].shape[0]

time: 874 us -> 1030 us (1.18)
  waiting for transfers between devices: 158 us -> 287 us
  blocking collectives: 0 us -> 19 us
  starting transfers between devices: 37.9 us -> 48.6 us
    all_gather x1, waiting for transfers between devices: 7.58 us -> 132 us  [per_device(): lax.all_gather(value_tiles, 'seq', axis=0, tiled=True)]
    all_to_all x1, waiting for transfers between devices: 0.01 us -> 94 us  [per_device(): lax.all_to_all(jnp.stack([key_tiles] * lax.axis_size('seq')), 'seq', 0, 0)]
    all_gather x1 -> x0, waiting for transfers between devices: 92.9 us -> none  [per_device(): lax.all_gather(key_tiles, 'seq', axis=0, tiled=True)]
    all_to_all x0 -> x1, blocking collectives: none -> 19 us  [per_device(): lax.all_to_all(jnp.take(key_tiles, far_out, axis=0), 'grp', split_axis=0,...]
  transfers between devices with their start and end apart: 8 -> 7, of which waited for: 4 -> 4; matrix products, arithmetic and copies ran while one was open for 47% -> 39% of each run, Pallas kernels for 0% -> 0%
where the time goes in v1:
time: 1030 us; the launch traced here: 1020 us
  waiting for transfers between devices  287 us (28%)
  other arithmetic  277 us (27%)
  local copies, waits for them, and re-layouts  252 us (24%)
  matrix products  119 us (12%)
  starting transfers between devices  48.6 us (5%)
  blocking collectives  19 us (2%)
  between operations  15.9 us (2%)
    scatter-add x24, other arithmetic, spread(): total.at[slot].add(jnp.where(chosen_pick, term, 0.0)).astype(jnp.bfloat16)  190 us
    all_gather x1, waiting for transfers between devices, per_device(): lax.all_gather(value_tiles, 'seq', axis=0, tiled=True)  132 us
    all_to_all x1, waiting for transfers between devices, per_device(): lax.all_to_all(jnp.stack([key_tiles] * lax.axis_size('seq')), 'seq', 0, 0)  94 us
    select_n x24, local copies, waits for them, and re-layouts, spread(): jnp.where(chosen_pick, term, 0.0)  72.8 us
    all_to_all x1, waiting for transfers between devices, per_device(): lax.all_to_all(joined(near_key_parts), 'seq', split_axis=0, concat_axis=0...  45.9 us
    gather x16, local copies, waits for them, and re-layouts, fetch(): from_far = jnp.take(columns_of(far_source), far_slot, axis=0)  36.5 us
    gather x16, local copies, waits for them, and re-layouts, fetch(): from_near = jnp.take(columns_of(near_source), near_slot, axis=0)  36.5 us
    select_n x1, other arithmetic, spread(): jnp.where(chosen_pick, term, 0.0)  32.1 us
  transfers between devices with their start and end apart: 7, of which 4 were waited for; matrix products, arithmetic and copies ran while one was open for 39% of the time, Pallas kernels for 0%

profile of v1, /device:TPU:1, one launch (start us, length us, event | category | flops | bytes accessed | tf_op | source)
XLA Modules:
  0.0 1020.2 jit_solution(17884636403731763918)
XLA Ops:
  12.9 6.8 all-to-all-start
  20.5 14.4 %all-to-all-done = bf16[8,128,512]{2,1,0:T(8,128)(2,1)S(1)} async-done(((bf16[8,128,512]{2,1,0:T(8,128)(2,1)}), bf16[8,128,512]{2,1,0:T(8,128)(2,1)S(1)}, u32[]{:S(2)}, u32[]{:S(2)}) %all-to-all-start) | async-done | bytes 1048608 | tf_op jit(solution)/shard_map/all_to_all | solution.py:85
  34.9 19.0 %all_to_all.35 = bf16[8,128,512]{2,1,0:T(8,128)(2,1)} all-to-all(bf16[8,128,512]{2,1,0:T(8,128)(2,1)S(1)} %get-tuple-element.166), channel_id=1, replica_groups=mesh['grp'=8,'seq'=32] {'grp'}, dimensions={0} | all-to-all | bytes 2097152 | tf_op jit(solution)/shard_map/all_to_all | solution.py:82
  53.9 6.1 stack.3
  60.0 11.1 %all-to-all-start.1 = ((bf16[32,3,128,512]{3,2,1,0:T(8,128)(2,1)}), bf16[32,3,128,512]{3,2,1,0:T(8,128)(2,1)}, u32[]{:S(2)}, u32[]{:S(2)}) async-start(bf16[32,3,128,512]{3,2,1,0:T(8,128)(2,1)} %stack.3), calls=%async_computation.1 | async-start | bytes 25165824 | tf_op jit(solution)/shard_map/all_to_all | solution.py:66
  157.4 132.4 %all-gather.3.cloned.1.call-done = bf16[1,96,1,128,512]{4,3,2,0,1:T(8,128)(2,1)} async-done(((bf16[1,3,1,128,512]{4,3,2,0,1:T(8,128)(2,1)}), bf16[1,96,1,128,512]{4,3,2,0,1:T(8,128)(2,1)}) %all-gather.3.cloned.1.call-update) | async-done | bytes 12582928 | tf_op jit(solution)/shard_map/all_gather | solution.py:68
  289.9 19.3 %fusion.28 = bf16[32,128,512]{2,0,1:T(8,128)(2,1)S(1)} fusion(bf16[1,96,1,128,512]{4,3,2,0,1:T(8,128)(2,1)} %all-gather.3.cloned.1.call-done, s32[96]{0:T(128)S(1)} %get-tuple-element.179, s32[96]{0:T(128)S(1)} %get-tuple-element.180, s32[32]{0:T(128)S(1)} %select_reduce_fusion), kind=kOutput, calls=%fused_computation.121 | convolution fusion | flops 404759552 | bytes 16778112 | tf_op jit(solution)/shard_map/pn,ntw->ptw/dot_general | solution.py:77
  316.3 94.0 %all-to-all-done.1 = bf16[32,3,128,512]{3,2,1,0:T(8,128)(2,1)} async-done(((bf16[32,3,128,512]{3,2,1,0:T(8,128)(2,1)}), bf16[32,3,128,512]{3,2,1,0:T(8,128)(2,1)}, u32[]{:S(2)}, u32[]{:S(2)}) %all-to-all-start.1) | async-done | bytes 12582944 | tf_op jit(solution)/shard_map/all_to_all | solution.py:66
  410.3 19.1 %fusion.25 = bf16[32,128,512]{2,0,1:T(8,128)(2,1)S(1)} fusion(bf16[96,128,512]{2,1,0:T(8,128)(2,1)} %bitcast.14, s32[96]{0:T(128)S(1)} %get-tuple-element.179, s32[96]{0:T(128)S(1)} %get-tuple-element.180, s32[32]{0:T(128)S(1)} %select_reduce_fusion), kind=kOutput, calls=%fused_computation.120 | convolution fusion | flops 404759552 | bytes 16778112 | tf_op jit(solution)/shard_map/pn,ntw->ptw/dot_general | solution.py:76
  473.6 8.8 fusion.34
  487.9 4.9 fusion.38
  492.8 6.2 fusion.17
  499.0 6.1 fusion.10
  505.1 4.0 fusion.12
  542.3 4.8 fusion.8
  566.8 32.1 %bitcast_select_fusion.18 = (f32[3,16,128,128]{2,3,1,0:T(8,128)}, f32[3,16,128,128]{2,3,1,0:T(8,128)}, f32[3,16,128,128]{2,3,1,0:T(8,128)}, f32[3,16,128,128]{2,...) fusion(f32[3,16,128,2,64]{2,4,3,1,0:T(8,128)S(1)} %copy.1019, ...), kind=kLoop, calls=%fused_computation.105 | loop fusion | flops 18874368 | bytes 100663440 | tf_op jit(solution)/shard_map/jit(_where)/select_n | solution.py:105
  602.5 7.1 scatter_fusion.11
  613.3 6.7 scatter_fusion.10
  624.4 6.7 scatter_fusion.9
  635.5 6.7 scatter_fusion.8
  644.6 5.6 all-to-all-start.4
  652.5 6.7 scatter_fusion.23
  662.9 6.7 scatter_fusion.22
  670.4 3.7 copy.1052
  674.1 6.7 scatter_fusion.21
  685.2 6.7 scatter_fusion.20
  694.3 5.1 all-to-all-start.6
  702.0 6.7 scatter_fusion.7
  712.6 6.7 scatter_fusion.6
  724.3 6.7 scatter_fusion.5
  735.9 6.7 scatter_fusion.4
  746.4 10.1 all-to-all-start.3
  759.2 6.7 scatter_fusion.19
  769.9 6.7 scatter_fusion.18
  781.6 6.7 scatter_fusion.17
  793.2 6.7 scatter_fusion.16
  803.8 45.9 %all-to-all-done.3 = bf16[32,128,512]{2,1,0:T(8,128)(2,1)} async-done(((bf16[32,128,512]{2,1,0:T(8,128)(2,1)}), bf16[32,128,512]{2,1,0:T(8,128)(2,1)}, u32[]{:S(2)}, u32[]{:S(2)}) %all-to-all-start.3) | async-done | bytes 4194336 | tf_op jit(solution)/shard_map/all_to_all | solution.py:186
  849.7 9.9 all-to-all-start.5
  880.6 10.2 %scatter_fusion.3 = f32[3,128,128]{2,1,0:T(8,128)} fusion(f32[3,128,128]{2,1,0:T(8,128)} %broadcast.259.clone, s32[48]{0:T(128)S(1)} %copy-done.42, f32[48,128,128]{2,1,0:T(8,128)S(1)} %copy.1020), kind=kCustom, calls=%fused_computation.31 | custom fusion | flops 786432 | bytes 9437376 | tf_op jit(solution)/shard_map/scatter-add | solution.py:105
  894.8 10.2 %scatter_fusion.2 = f32[3,128,128]{2,1,0:T(8,128)} fusion(f32[3,128,128]{2,1,0:T(8,128)} %broadcast.259.clone.1, s32[48]{0:T(128)S(1)} %copy-done.42, f32[48,128,128]{2,1,0:T(8,128)S(1)} %copy.1017), kind=kCustom, calls=%fused_computation.30 | custom fusion | flops 786432 | bytes 9437376 | tf_op jit(solution)/shard_map/scatter-add | solution.py:105
  909.1 10.2 %scatter_fusion.1 = f32[3,128,128]{2,1,0:T(8,128)} fusion(f32[3,128,128]{2,1,0:T(8,128)} %broadcast.259.clone.2, s32[48]{0:T(128)S(1)} %copy-done.42, f32[48,128,128]{2,1,0:T(8,128)S(1)} %copy.1014), kind=kCustom, calls=%fused_computation.29 | custom fusion | flops 786432 | bytes 9437376 | tf_op jit(solution)/shard_map/scatter-add | solution.py:105
  923.3 10.2 %scatter_fusion = f32[3,128,128]{2,1,0:T(8,128)} fusion(f32[3,128,128]{2,1,0:T(8,128)} %broadcast.259.clone.3, s32[48]{0:T(128)S(1)} %copy-done.42, f32[48,128,128]{2,1,0:T(8,128)S(1)} %copy.1011), kind=kCustom, calls=%fused_computation.28 | custom fusion | flops 786432 | bytes 9437376 | tf_op jit(solution)/shard_map/scatter-add | solution.py:105
  938.2 10.2 %scatter_fusion.15 = f32[3,128,128]{2,1,0:T(8,128)} fusion(f32[3,128,128]{2,1,0:T(8,128)} %broadcast.259.clone.4, s32[48]{0:T(128)S(1)} %copy-done.42, f32[48,128,128]{2,1,0:T(8,128)S(1)} %copy.1044), kind=kCustom, calls=%fused_computation.43 | custom fusion | flops 786432 | bytes 9437376 | tf_op jit(solution)/shard_map/scatter-add | solution.py:105
  952.4 10.2 %scatter_fusion.14 = f32[3,128,128]{2,1,0:T(8,128)} fusion(f32[3,128,128]{2,1,0:T(8,128)} %broadcast.259.clone.5, s32[48]{0:T(128)S(1)} %copy-done.42, f32[48,128,128]{2,1,0:T(8,128)S(1)} %copy.1041), kind=kCustom, calls=%fused_computation.42 | custom fusion | flops 786432 | bytes 9437376 | tf_op jit(solution)/shard_map/scatter-add | solution.py:105
  967.3 10.2 %scatter_fusion.13 = f32[3,128,128]{2,1,0:T(8,128)} fusion(f32[3,128,128]{2,1,0:T(8,128)} %broadcast.259.clone.6, s32[48]{0:T(128)S(1)} %copy-done.42, f32[48,128,128]{2,1,0:T(8,128)S(1)} %copy.1038), kind=kCustom, calls=%fused_computation.41 | custom fusion | flops 786432 | bytes 9437376 | tf_op jit(solution)/shard_map/scatter-add | solution.py:105
  982.4 10.2 %scatter_fusion.12 = f32[3,128,128]{2,1,0:T(8,128)} fusion(f32[3,128,128]{2,1,0:T(8,128)} %broadcast.259.clone.7, s32[48]{0:T(128)S(1)} %copy-done.42, f32[48,128,128]{2,1,0:T(8,128)S(1)} %copy.1035), kind=kCustom, calls=%fused_computation.40 | custom fusion | flops 786432 | bytes 9437376 | tf_op jit(solution)/shard_map/scatter-add | solution.py:105
  1001.2 4.6 fusion.23
  1007.0 4.6 fusion.21
  (376 shorter events, 335.9 us)
Async XLA Ops:
  7.2 3.9 copy-start.13
  12.9 41.0 %copy-start.12 = (bf16[1,3,1,128,512]{4,3,2,1,0:T(8,128)(2,1)S(1)}, bf16[1,3,1,128,512]{4,3,2,1,0:T(8,128)(2,1)}, u32[]{:S(2)}) copy-start(bf16[1,3,1,128,512]{4,3,2,1,0:T(8,128)(2,1)} %param.17) | copy-start | bytes 1179652
  12.9 21.9 %all-to-all-start = ((bf16[8,128,512]{2,1,0:T(8,128)(2,1)}), bf16[8,128,512]{2,1,0:T(8,128)(2,1)S(1)}, u32[]{:S(2)}, u32[]{:S(2)}) async-start(bf16[8,128,512]{2,1,0:T(8,128)(2,1)} %get-tuple-element.167), calls=%async_computation | async-start | bytes 2097152 | tf_op jit(solution)/shard_map/all_to_all | solution.py:85
  19.7 270.1 %all-gather.3.cloned.1.call-start = ((), (), s32[]{:S(2)}) async-start(), calls=%async_computation.7 | async-start | bytes 12976128 | tf_op jit(solution)/shard_map/all_gather | solution.py:68
  34.9 25.1 %copy-start.25 = (bf16[8,128,512]{2,1,0:T(8,128)(2,1)}, bf16[8,128,512]{2,1,0:T(8,128)(2,1)S(1)}, u32[]{:S(2)}) copy-start(bf16[8,128,512]{2,1,0:T(8,128)(2,1)S(1)} %all-to-all-done) | copy-start | bytes 3145732
  60.0 11.1 %copy-start.55 = (s32[768,16]{0,1:T(8,128)S(1)}, s32[768,16]{0,1:T(8,128)}, u32[]{:S(2)}) copy-start(s32[768,16]{0,1:T(8,128)} %param.20) | copy-start | bytes 147460
  60.0 11.3 %copy-start.52 = (bf16[1,3,1,128,512]{4,3,2,1,0:T(8,128)(2,1)S(1)}, bf16[1,3,1,128,512]{4,3,2,1,0:T(8,128)(2,1)}, u32[]{:S(2)}) copy-start(bf16[1,3,1,128,512]{4,3,2,1,0:T(8,128)(2,1)} %param.19) | copy-start | bytes 1179652
  60.0 12.8 %copy-start.64 = (s32[768,16]{0,1:T(8,128)S(1)}, s32[768,16]{0,1:T(8,128)}, u32[]{:S(2)}) copy-start(s32[768,16]{0,1:T(8,128)} %param.21) | copy-start | bytes 147460
  60.0 350.3 %all-to-all-start.1 = ((bf16[32,3,128,512]{3,2,1,0:T(8,128)(2,1)}), bf16[32,3,128,512]{3,2,1,0:T(8,128)(2,1)}, u32[]{:S(2)}, u32[]{:S(2)}) async-start(bf16[32,3,128,512]{3,2,1,0:T(8,128)(2,1)} %stack.3), calls=%async_computation.1 | async-start | bytes 25165824 | tf_op jit(solution)/shard_map/all_to_all | solution.py:66
  71.1 6.9 copy-start.14
  76.7 408.6 %copy-start.67 = (pred[3,16]{1,0:T(4,128)(4,1)}, pred[3,16]{1,0:T(4,128)(4,1)S(1)}, u32[]{:S(2)}) copy-start(pred[3,16]{1,0:T(4,128)(4,1)S(1)} %get-tuple-element.61) | copy-start | bytes 148
  77.2 408.0 %copy-start.65 = (pred[3,16]{1,0:T(4,128)(4,1)}, pred[3,16]{1,0:T(4,128)(4,1)S(1)}, u32[]{:S(2)}) copy-start(pred[3,16]{1,0:T(4,128)(4,1)S(1)} %get-tuple-element.69) | copy-start | bytes 148
  77.3 39.0 %copy-start.45 = (s32[48]{0:T(128)}, s32[48]{0:T(128)S(1)}, u32[]{:S(2)}) copy-start(s32[48]{0:T(128)S(1)} %reshape.883) | copy-start | bytes 580
  77.4 38.9 %copy-start.43 = (s32[48]{0:T(128)}, s32[48]{0:T(128)S(1)}, u32[]{:S(2)}) copy-start(s32[48]{0:T(128)S(1)} %reshape.877) | copy-start | bytes 580
  95.8 386.6 %copy-start.37 = (bf16[3,128,128]{1,2,0:T(8,128)(2,1)}, bf16[3,128,128]{1,2,0:T(8,128)(2,1)S(1)}, u32[]{:S(2)}) copy-start(bf16[3,128,128]{1,2,0:T(8,128)(2,1)S(1)} %copy.969) | copy-start | bytes 294916
  107.4 8.1 copy-start.53
  108.2 6.5 copy-start.54
  487.9 4.9 copy-start.47
  492.8 6.3 copy-start.15
  492.8 6.3 copy-start.16
  492.8 6.2 copy-start.30
  492.8 6.2 copy-start.48
  505.1 4.0 copy-start.36
  505.1 4.0 copy-start.57
  518.8 28.2 %copy-start.4 = (bf16[3,2,128,16,128]{2,4,3,1,0:T(8,128)(2,1)}, bf16[3,2,128,16,128]{2,4,3,1,0:T(8,128)(2,1)S(1)}, u32[]{:S(2)}) copy-start(bf16[3,2,128,16,128]{2,4,3,1,0:T(8,128)(2,1)S(1)} %fusion.5) | copy-start | bytes 9437188
  527.2 36.5 %copy-start.5 = (bf16[3,2,128,16,128]{2,4,3,1,0:T(8,128)(2,1)}, bf16[3,2,128,16,128]{2,4,3,1,0:T(8,128)(2,1)S(1)}, u32[]{:S(2)}) copy-start(bf16[3,2,128,16,128]{2,4,3,1,0:T(8,128)(2,1)S(1)} %fusion.6) | copy-start | bytes 9437188
  530.2 6.5 slice-start
  536.7 23.9 %copy-start.6 = (bf16[3,2,128,16,128]{2,4,3,1,0:T(8,128)(2,1)}, bf16[3,2,128,16,128]{2,4,3,1,0:T(8,128)(2,1)S(1)}, u32[]{:S(2)}) copy-start(bf16[3,2,128,16,128]{2,4,3,1,0:T(8,128)(2,1)S(1)} %fusion.7) | copy-start | bytes 9437188
  542.3 4.8 copy-start.40
  547.1 10.4 %copy-start.7 = (bf16[3,2,128,16,128]{2,4,3,1,0:T(8,128)(2,1)}, bf16[3,2,128,16,128]{2,4,3,1,0:T(8,128)(2,1)S(1)}, u32[]{:S(2)}) copy-start(bf16[3,2,128,16,128]{2,4,3,1,0:T(8,128)(2,1)S(1)} %fusion.8) | copy-start | bytes 9437188
  642.3 7.9 copy-start.11
  644.6 49.7 %all-to-all-start.4 = ((bf16[8,128,512]{2,1,0:T(8,128)(2,1)}), bf16[8,128,512]{2,1,0:T(8,128)(2,1)}, u32[]{:S(2)}, u32[]{:S(2)}) async-start(bf16[8,128,512]{2,1,0:T(8,128)(2,1)} %pad_maximum_fusion.2), calls=%async_computation.4 | async-start | bytes 2097152 | tf_op jit(solution)/shard_map/all_to_all | solution.py:190
  691.9 7.4 copy-start.10
  694.3 52.2 %all-to-all-start.6 = ((bf16[8,128,512]{2,1,0:T(8,128)(2,1)}), bf16[8,128,512]{2,1,0:T(8,128)(2,1)}, u32[]{:S(2)}, u32[]{:S(2)}) async-start(bf16[8,128,512]{2,1,0:T(8,128)(2,1)} %pad_maximum_fusion.3), calls=%async_computation.6 | async-start | bytes 2097152 | tf_op jit(solution)/shard_map/all_to_all | solution.py:191
  746.4 10.1 copy-start.9
  746.4 103.3 %all-to-all-start.3 = ((bf16[32,128,512]{2,1,0:T(8,128)(2,1)}), bf16[32,128,512]{2,1,0:T(8,128)(2,1)}, u32[]{:S(2)}, u32[]{:S(2)}) async-start(bf16[32,128,512]{2,1,0:T(8,128)(2,1)} %pad_maximum_fusion), calls=%async_computation.3 | async-start | bytes 8388608 | tf_op jit(solution)/shard_map/all_to_all | solution.py:186
  803.8 57.0 %copy-start.56 = (bf16[3,2,64,128]{3,2,1,0:T(8,128)(2,1)S(1)}, bf16[3,2,64,128]{3,2,1,0:T(8,128)(2,1)}, u32[]{:S(2)}) copy-start(bf16[3,2,64,128]{3,2,1,0:T(8,128)(2,1)} %get-tuple-element.172) | copy-start | bytes 294916
  803.8 57.8 %copy-start.58 = (bf16[3,2,64,128]{3,2,1,0:T(8,128)(2,1)S(1)}, bf16[3,2,64,128]{3,2,1,0:T(8,128)(2,1)}, u32[]{:S(2)}) copy-start(bf16[3,2,64,128]{3,2,1,0:T(8,128)(2,1)} %get-tuple-element.174) | copy-start | bytes 294916
  803.8 58.5 %copy-start.59 = (bf16[3,2,64,128]{3,2,1,0:T(8,128)(2,1)S(1)}, bf16[3,2,64,128]{3,2,1,0:T(8,128)(2,1)}, u32[]{:S(2)}) copy-start(bf16[3,2,64,128]{3,2,1,0:T(8,128)(2,1)} %get-tuple-element.176) | copy-start | bytes 294916
  803.8 59.3 %copy-start.60 = (bf16[3,2,64,128]{3,2,1,0:T(8,128)(2,1)S(1)}, bf16[3,2,64,128]{3,2,1,0:T(8,128)(2,1)}, u32[]{:S(2)}) copy-start(bf16[3,2,64,128]{3,2,1,0:T(8,128)(2,1)} %get-tuple-element.178) | copy-start | bytes 294916
  803.8 60.0 %copy-start.3 = (bf16[3,16,128,128]{2,3,1,0:T(8,128)(2,1)S(1)}, bf16[3,16,128,128]{2,3,1,0:T(8,128)(2,1)}, u32[]{:S(2)}) copy-start(bf16[3,16,128,128]{2,3,1,0:T(8,128)(2,1)} %copy-done.2) | copy-start | bytes 4718596
  849.7 157.3 %all-to-all-start.5 = ((bf16[32,128,512]{2,1,0:T(8,128)(2,1)}), bf16[32,128,512]{2,1,0:T(8,128)(2,1)}, u32[]{:S(2)}, u32[]{:S(2)}) async-start(bf16[32,128,512]{2,1,0:T(8,128)(2,1)} %pad_maximum_fusion.1), calls=%async_computation.5 | async-start | bytes 8388608 | tf_op jit(solution)/shard_map/all_to_all | solution.py:187
  859.7 7.5 copy-start.1
  869.8 4.8 copy-start.8
  982.4 14.8 %copy-start.70 = (s32[8]{0:T(128)S(1)}, s32[8]{0:T(128)}, u32[]{:S(2)}) copy-start(s32[8]{0:T(128)} %copy-done.69) | copy-start | bytes 100
  1001.2 4.6 copy-start.49
  1007.0 4.7 copy-start.50
  1007.0 4.7 copy-start.51
  (33 other events, 75.9 us)
Sparse Core Ops, SparseCore 0:
  23.1 266.6 all-gather.2
